TPU v7x, 32 devices: a whole 2x2x4 slice. The times are simulated.
32 devices in a mesh: parts: 2 (over y), tile: 4 (over x, core), chan: 4 (over z).
Axes of the slice: x: 2, y: 2, z: 4, core: 2. Of those that a mesh axis runs over, the one named last changes fastest.
Arguments:
- weather: bfloat16 [768, 64, 1440], P('chan', 'parts', 'tile'), parts along dimension 1, may hold values from -6 to 6
- lon_taps: float32 [9, 768], P(None, 'chan'), may hold values from -4 to 4
- latitude_taps: float32 [9, 768], P(None, 'chan'), may hold values from -2 to 2
- norm_gain: float32 [768], replicated, may hold values from 0.1 to 1.9
- up_weight: bfloat16 [768, 3072], P(None, ('tile', 'chan')), may hold values from -0.21875 to 0.21875
- down_weight: bfloat16 [768, 3072], P(None, ('tile', 'chan')), may hold values from -0.109375 to 0.109375
Outputs:
- mixed: bfloat16 [768, 64, 1440], P('chan', 'parts', 'tile'), parts along dimension 1
There are 2 independent parts, one for each index of `parts`. A program takes and returns all parts, laid end to end along the dimension named above; an argument that names none is the same for every part. Nothing has to cross between parts.
All inputs are finite; a program needn't handle non-finite values.
Results may differ from a plain program's by a relative error of at most 0.0065.
Values may be sent and summed in bfloat16 or wider, within the bound.
No kernel may reach another device: no remote copies, remote signals or barrier semaphores. Data moves between devices by JAX's collectives and lax.ppermute only.
A program may use at most 128 MiB of HBM per device.

v0:
```python
import jax
import jax.numpy as jnp
from jax import lax
from jax.sharding import PartitionSpec as P

KERNEL_TAPS = 9
DILATION_STEP = 2


def with_halo(shard, sides, width):
    for axis, dim in sides:
        devices, length = (lax.axis_size(axis), shard.shape[dim])
        up = [(i, (i + 1) % devices) for i in range(devices)]
        down = [(j, i) for i, j in up]
        last = lax.slice_in_dim(shard, length - width, length, axis=dim)
        initial = lax.slice_in_dim(shard, 0, width, axis=dim)
        before = lax.ppermute(last, axis, up)
        after = lax.ppermute(initial, axis, down)
        shard = jnp.concatenate([before, shard, after], axis=dim)
    return shard


def layer_norm(values, norm_gain):
    as_float = values.astype(jnp.float32)
    center = jnp.mean(as_float, axis=0)
    deviation = as_float - center
    spread_sq = jnp.mean(deviation * deviation, axis=0)
    return (deviation * lax.rsqrt(spread_sq + 1e-06) * norm_gain[:, None]).astype(jnp.bfloat16)


def on_device(weather, lon_taps, latitude_taps, norm_gain, up_weight, down_weight):
    chan_count, row_total, column_total = weather.shape
    border_width = DILATION_STEP * (KERNEL_TAPS // 2)
    widened_field = with_halo(weather, (("tile", 2),), border_width)
    lon_sum = jnp.zeros(weather.shape, jnp.float32)
    for kernel_tap_index in range(KERNEL_TAPS):
        sliding_window = widened_field[
            :, :, DILATION_STEP * kernel_tap_index : DILATION_STEP * kernel_tap_index + column_total
        ].astype(jnp.float32)
        lon_sum = lon_sum + lon_taps[kernel_tap_index][:, None, None] * sliding_window
    padded_field = jnp.pad(lon_sum, ((0, 0), (border_width, border_width), (0, 0)))
    latitude_sum = jnp.zeros(weather.shape, jnp.float32)
    for kernel_tap_index in range(KERNEL_TAPS):
        latitude_sum = (
            latitude_sum
            + latitude_taps[kernel_tap_index][:, None, None]
            * padded_field[
                :,
                DILATION_STEP * kernel_tap_index : DILATION_STEP * kernel_tap_index + row_total,
                :,
            ]
        )
    spatial = latitude_sum.astype(jnp.bfloat16)
    group_count = lax.axis_size("chan")
    width_all = chan_count * group_count
    shard_width = up_weight.shape[1]
    by_cell = lax.all_to_all(spatial, "chan", split_axis=1, concat_axis=0, tiled=True)
    cell_count = by_cell.shape[1] * by_cell.shape[2]
    normed = layer_norm(by_cell.reshape(width_all, cell_count), norm_gain)
    expanded = lax.dot_general(
        lax.all_gather(up_weight, ("tile", "chan"), axis=1, tiled=True),
        normed,
        (((0,), (0,)), ((), ())),
        preferred_element_type=jnp.float32,
    )
    hidden = jax.nn.gelu(expanded, approximate=False).astype(jnp.bfloat16)
    down_all = lax.all_gather(down_weight, ("tile", "chan"), axis=1, tiled=True)
    tile_count = down_all.shape[1] // (group_count * shard_width)
    down_groups = down_all.reshape(width_all, tile_count, group_count, shard_width)
    hidden_groups = hidden.reshape(tile_count, group_count, shard_width, cell_count)
    summed = jnp.zeros((width_all, cell_count), jnp.float32)
    for group in range(group_count):
        group_value = jnp.einsum(
            "dts,tsc->dc",
            down_groups[:, :, group, :],
            hidden_groups[:, group],
            preferred_element_type=jnp.float32,
        ).astype(jnp.bfloat16)
        group_value = lax.optimization_barrier(group_value)
        summed = summed + group_value.astype(jnp.float32)
    update_cells = summed.astype(jnp.bfloat16).reshape(width_all, by_cell.shape[1], column_total)
    update = lax.all_to_all(update_cells, "chan", split_axis=0, concat_axis=1, tiled=True)
    return (weather.astype(jnp.float32) + update.astype(jnp.float32)).astype(jnp.bfloat16)


def solution(mesh):
    return jax.shard_map(
        on_device,
        mesh=mesh,
        in_specs=(
            P("chan", "parts", "tile"),
            P(None, "chan"),
            P(None, "chan"),
            P(),
            P(None, ("tile", "chan")),
            P(None, ("tile", "chan")),
        ),
        out_specs=P("chan", "parts", "tile"),
        check_vma=False,
    )
```

profile of v0, /device:TPU:0, one launch (start us, length us, event | category | flops | bytes accessed | tf_op | source)
XLA Modules:
  0.0 563.3 jit_solution(12894988400171444290)
XLA Ops:
  6.5 0.0 copy-start.1
  6.5 0.0 copy-start.2
  6.5 0.0 all-gather.3.cloned.1.call-start
  6.5 0.7 all-gather.3.cloned.1.call-update
  7.3 2.6 fusion.56
  9.9 1.3 copy.53
  11.2 2.4 collective-permute-start.1
  13.6 1.3 copy.52
  14.9 0.1 collective-permute-start
  14.9 0.0 copy-done.1
  14.9 0.0 copy-done.2
  15.0 4.3 collective-permute-done
  19.3 1.3 copy.36
  20.6 0.0 collective-permute-done.1
  20.6 1.3 copy.38
  22.0 36.4 %fusion.22 = f32[192,32,360]{2,1,0:T(8,128)} fusion(bf16[192,32,360]{2,1,0:T(8,128)(2,1)} %param.6, bf16[192,32,8]{2,1,0:T(8,128)(2,1)S(1)} %copy.38, bf16[192,32,8]{2,1,0:T(8,128)(2,1)S(1)} %copy.36, f32[192]{0:T(256)S(1)} %bitcast.205, f32[192]{0:T(256)S(1)} %bitcast.206, f32[192]{0:T(256)S(1)} %bitcast.199, f32[192]{0:T(256)S(1)} %bitcast.200, ...), kind=kLoop, calls=%fused_computation.38 | loop fusion | flops 110592000 | bytes 13474560 | tf_op jit(solution)/shard_map/add | solution.py:40
  58.4 34.3 %fusion.33 = bf16[192,32,360]{2,1,0:T(8,128)(2,1)S(1)} fusion(f32[192,32,360]{2,1,0:T(8,128)} %fusion.22, f32[192]{0:T(256)S(1)} %bitcast.196, f32[192]{0:T(256)S(1)} %bitcast.197, f32[192]{0:T(256)S(1)} %bitcast.190, f32[192]{0:T(256)S(1)} %bitcast.191, f32[192]{0:T(256)S(1)} %bitcast.192, f32[192]{0:T(256)S(1)} %bitcast.193, f32[192]{0:T(256)S(1)} %bitcast.194, ...), kind=kLoop, calls=%fused_computation.49 | loop fusion | flops 39813120 | bytes 13277952 | tf_op jit(solution)/shard_map/convert_element_type | solution.py:53
  92.7 4.0 copy.39
  96.7 5.0 all-to-all-start
  101.6 0.3 all-gather.5.cloned.1.call-start
  101.9 0.4 all-gather.5.cloned.1.call-update
  102.4 130.9 %all-to-all-done = bf16[192,32,360]{2,0,1:T(8,128)(2,1)} async-done(((bf16[192,32,360]{2,0,1:T(8,128)(2,1)}), bf16[192,32,360]{2,0,1:T(8,128)(2,1)}, u32[]{:S(2)}, u32[]{:S(2)}) %all-to-all-start) | async-done | bytes 4423712 | tf_op jit(solution)/shard_map/all_to_all | solution.py:57
  233.2 3.5 bitcast_convert_fusion.4
  236.7 5.0 fusion.55
  241.7 9.1 %copy.68 = f32[192,4,8,360]{3,2,0,1:T(8,128)} copy(f32[192,4,8,360]{3,0,2,1:T(8,128)S(1)} %bitcast_convert_fusion.4) | data formatting | bytes 17694720 | tf_op jit(solution)/shard_map/convert_element_type | solution.py:24
  250.8 5.0 multiply_reduce_fusion
  255.8 0.0 copy-start.3
  255.9 0.1 div.9
  255.9 11.5 %reshape.71 = f32[768,2880]{1,0:T(8,128)} reshape(f32[4,192,8,360]{3,2,1,0:T(8,128)} %bitcast.180) | data formatting | bytes 17694720 | tf_op jit(solution)/shard_map/convert_element_type | solution.py:24
  267.4 0.1 rsqrt.11
  267.5 0.0 copy-done.3
  267.5 7.2 %multiply_convert_fusion.1.clone.4 = bf16[768,2880]{1,0:T(8,128)(2,1)} fusion(f32[768,2880]{1,0:T(8,128)} %reshape.71, f32[768]{0:T(1024)S(1)} %copy-done.3, f32[2880]{0:T(1024)S(1)} %rsqrt.11, f32[2880]{0:T(1024)S(1)} %div.9), kind=kLoop, calls=%fused_computation.60.clone.clone.clone.clone.1 | loop fusion | flops 8847360 | bytes 13297152 | tf_op jit(solution)/shard_map/convert_element_type | solution.py:66
  274.7 0.0 all-gather.3.cloned.1.call-done
  274.7 102.8 %fusion.2 = bf16[3072,2880]{0,1:T(8,128)(2,1)} fusion(bf16[768,3072]{0,1:T(8,128)(2,1)} %all-gather.3.cloned.1.call-done, bf16[768,2880]{1,0:T(8,128)(2,1)} %multiply_convert_fusion.1.clone.4), kind=kOutput, calls=%fused_computation.3 | convolution fusion | flops 14164623360 | bytes 26836992 | tf_op jit(solution)/shard_map/dot_general | solution.py:60
  377.5 22.1 %copy.41 = bf16[3072,2880]{1,0:T(8,128)(2,1)} copy(bf16[3072,2880]{0,1:T(8,128)(2,1)} %fusion.2) | data formatting | bytes 35389440 | tf_op jit(solution)/shard_map/convert_element_type | solution.py:66
  399.7 0.0 all-gather.5.cloned.1.call-done
  399.7 8.7 %fusion.53 = bf16[768,2880]{0,1:T(8,128)(2,1)} fusion(bf16[4,4,192,2880]{3,2,1,0:T(8,128)(2,1)} %bitcast.184, bf16[768,4,4,192]{0,3,2,1:T(8,128)(2,1)} %bitcast.207), kind=kOutput, calls=%fused_computation.92 | convolution fusion | flops 3399598080 | bytes 10125312 | tf_op jit(solution)/shard_map/dts,tsc->dc/dot_general | solution.py:73
  408.4 0.1 copy-done
  408.5 1.9 copy-done.4
  410.5 5.5 fusion.52
  415.9 5.6 fusion.51
  421.5 5.7 %fusion.54 = bf16[768,2880]{0,1:T(8,128)(2,1)} fusion(bf16[4,4,192,2880]{3,2,1,0:T(8,128)(2,1)S(1)} %bitcast.187, bf16[768,4,4,192]{0,3,2,1:T(8,128)(2,1)S(1)} %bitcast.210), kind=kOutput, calls=%fused_computation.93 | convolution fusion | flops 3399598080 | bytes 10125312 | tf_op jit(solution)/shard_map/dts,tsc->dc/dot_general | solution.py:73
  427.2 10.3 %add_convert_fusion = bf16[768,2880]{0,1:T(8,128)(2,1)} fusion(bf16[768,2880]{0,1:T(8,128)(2,1)} %fusion.54, bf16[768,2880]{0,1:T(8,128)(2,1)} %fusion.53, bf16[768,2880]{0,1:T(8,128)(2,1)} %fusion.52, bf16[768,2880]{0,1:T(8,128)(2,1)} %fusion.51), kind=kLoop, calls=%fused_computation.65 | loop fusion | flops 17694720 | bytes 22118400 | tf_op jit(solution)/shard_map/convert_element_type | solution.py:81
  437.6 7.0 %copy.50 = bf16[768,8,360]{2,1,0:T(8,128)(2,1)} copy(bf16[768,8,360]{0,2,1:T(8,128)(2,1)} %bitcast.188) | data formatting | bytes 8847360 | tf_op jit(solution)/shard_map/reshape | solution.py:81
  444.5 108.1 %all_to_all.8 = bf16[768,8,360]{2,1,0:T(8,128)(2,1)S(1)} all-to-all(bf16[768,8,360]{2,1,0:T(8,128)(2,1)} %copy.50), channel_id=1, replica_groups=mesh['parts'=2,'tile'=4,'chan'=4] {'chan'}, dimensions={0} | all-to-all | bytes 8847360 | tf_op jit(solution)/shard_map/all_to_all | solution.py:82
  552.7 0.0 slice-done
  552.7 0.0 slice-done.1
  552.7 3.4 fusion.23
  (9 shorter events, 0.0 us)
Async XLA Ops:
  6.5 8.4 %copy-start.1 = (f32[9,192]{1,0:T(8,128)S(1)}, f32[9,192]{1,0:T(8,128)}, u32[]{:S(2)}) copy-start(f32[9,192]{1,0:T(8,128)} %param.7) | copy-start | bytes 20740
  6.5 8.4 %copy-start.2 = (f32[9,192]{1,0:T(8,128)S(1)}, f32[9,192]{1,0:T(8,128)}, u32[]{:S(2)}) copy-start(f32[9,192]{1,0:T(8,128)} %param.8) | copy-start | bytes 20740
  6.5 268.1 %all-gather.3.cloned.1.call-start = ((), (), s32[]{:S(2)}) async-start(), calls=%async_computation.2 | async-start | bytes 5013504 | tf_op jit(solution)/shard_map/all_gather | solution.py:61
  11.2 9.5 %collective-permute-start.1 = (bf16[192,32,8]{0,2,1:T(8,128)(2,1)S(1)}, bf16[192,32,8]{0,2,1:T(8,128)(2,1)S(1)}, u32[]{:S(2)}, u32[]{:S(2)}) collective-permute-start(bf16[192,32,8]{0,2,1:T(8,128)(2,1)S(1)} %copy.53), channel_id=1, source_target_pairs={{4,0},{8,4},{12,8},{0,12},{5,1},{9,5},{13,9},{1,13},{6,2},{10,6},{... | collective-permute-start | bytes 294920 | tf_op jit(solution)/shard_map/ppermute | solution.py:18
  14.9 4.4 collective-permute-start
  96.7 136.6 %all-to-all-start = ((bf16[192,32,360]{2,0,1:T(8,128)(2,1)}), bf16[192,32,360]{2,0,1:T(8,128)(2,1)}, u32[]{:S(2)}, u32[]{:S(2)}) async-start(bf16[192,32,360]{2,0,1:T(8,128)(2,1)} %copy.39), calls=%async_computation | async-start | bytes 9437184 | tf_op jit(solution)/shard_map/all_to_all | solution.py:57
  101.6 298.0 %all-gather.5.cloned.1.call-start = ((), (), s32[]{:S(2)}) async-start(), calls=%async_computation.3 | async-start | bytes 5013504 | tf_op jit(solution)/shard_map/all_gather | solution.py:67
  255.8 11.7 %copy-start.3 = (f32[768]{0:T(1024)S(1)}, f32[768]{0:T(1024)}, u32[]{:S(2)}) copy-start(f32[768]{0:T(1024)} %param.9) | copy-start | bytes 9220
  399.7 8.8 %copy-start = (bf16[3072,2880]{1,0:T(8,128)(2,1)S(1)}, bf16[3072,2880]{1,0:T(8,128)(2,1)}, u32[]{:S(2)}) copy-start(bf16[3072,2880]{1,0:T(8,128)(2,1)} %copy.41) | copy-start | bytes 53084164
  399.7 10.8 %copy-start.4 = (bf16[768,3072]{0,1:T(8,128)(2,1)S(1)}, bf16[768,3072]{0,1:T(8,128)(2,1)}, u32[]{:S(2)}) copy-start(bf16[768,3072]{0,1:T(8,128)(2,1)} %all-gather.5.cloned.1.call-done) | copy-start | bytes 14155780
  437.6 115.1 %slice-start = ((s8[4718592]{0:T(1024)(128)(4,1)}), s8[524288]{0:T(1024)(128)(4,1)S(1)}, s32[]{:S(2)}) async-start(s8[4718592]{0:T(1024)(128)(4,1)} %bitcast.181), calls=%async_computation.4 | async-start | bytes 1048576
  444.5 108.1 %slice-start.1 = ((s8[4718592]{0:T(1024)(128)(4,1)}), s8[4194304]{0:T(1024)(128)(4,1)S(1)}, s32[]{:S(2)}) async-start(s8[4718592]{0:T(1024)(128)(4,1)} %bitcast.181), calls=%async_computation.5 | async-start | bytes 8388608
Sparse Core Ops, SparseCore 0:
  9.7 56.0 all-gather.2
  104.8 103.3 all-gather.4
where the time goes:
time: 572 us; the launch traced here: 563 us
  waiting for transfers between devices  136 us (24%)
  matrix products  128 us (22%)
  blocking collectives  108 us (19%)
  other arithmetic  105 us (18%)
  local copies, waits for them, and re-layouts  63.8 us (11%)
  between operations  14 us (2%)
  starting transfers between devices  7.74 us (1%)
    all_to_all x1, waiting for transfers between devices, on_device(): lax.all_to_all(spatial, 'chan', split_axis=1, concat_axis=0, tiled=True)  131 us
    all_to_all x1, blocking collectives, on_device(): lax.all_to_all(update_cells, 'chan', split_axis=0, concat_axis=1, tiled=T...  108 us
    dot_general x1, matrix products, on_device(): lax.dot_general(lax.all_gather(up_weight, ('tile', 'chan'), axis=1, tiled...  103 us
    add x1, other arithmetic, on_device(): lon_sum + lon_taps[kernel_tap_index][:, None, None] * sliding_window  36.4 us
    convert_element_type x1, other arithmetic, on_device(): spatial = latitude_sum.astype(jnp.bfloat16)  34.3 us
    dot_general x4, matrix products, on_device(): jnp.einsum('dts,tsc->dc', down_groups[:, :, group, :], hidden_groups[:, g...  25.5 us
    convert_element_type x1, local copies, waits for them, and re-layouts, on_device(): hidden = jax.nn.gelu(expanded, approximate=False).astype(jnp.bfloat16)  22.1 us
    convert_element_type x2, local copies, waits for them, and re-layouts, layer_norm(): as_float = values.astype(jnp.float32)  20.6 us
  transfers between devices with their start and end apart: 5, of which 2 were waited for; matrix products, arithmetic and copies ran while one was open for 44% of the time, Pallas kernels for 0%

commit v1 on v0

--- a/solution.py
+++ b/solution.py
@@ -79,7 +79,19 @@
         group_value = lax.optimization_barrier(group_value)
         summed = summed + group_value.astype(jnp.float32)
     update_cells = summed.astype(jnp.bfloat16).reshape(width_all, by_cell.shape[1], column_total)
-    update = lax.all_to_all(update_cells, "chan", split_axis=0, concat_axis=1, tiled=True)
+    ways, here = (lax.axis_size("chan"), lax.axis_index("chan"))
+    width_2 = update_cells.shape[0] // ways
+    shape = list(update_cells.shape)
+    shape[0] = width_2
+    height = shape[1]
+    shape[1] = height * ways
+    full = jnp.zeros(shape, update_cells.dtype)
+    for mask in range(ways):
+        part = lax.dynamic_slice_in_dim(update_cells, (here ^ mask) * width_2, width_2, axis=0)
+        if mask:
+            part = lax.ppermute(part, "chan", [(d, d ^ mask) for d in range(ways)])
+        full = lax.dynamic_update_slice_in_dim(full, part, (here ^ mask) * height, axis=1)
+    update = full
     return (weather.astype(jnp.float32) + update.astype(jnp.float32)).astype(jnp.bfloat16)
 
 

time: 572 us -> 545 us (0.953)
  the two profiles are of different devices: /device:TPU:0 before, /device:TPU:8 now
where the time goes in v1:
time: 545 us; the launch traced here: 535 us
  waiting for transfers between devices  211 us (39%)
  matrix products  118 us (22%)
  local copies, waits for them, and re-layouts  90.3 us (17%)
  other arithmetic  76.7 us (14%)
  starting transfers between devices  25.1 us (5%)
  between operations  13.9 us (3%)
    all_to_all x1, waiting for transfers between devices, on_device(): lax.all_to_all(spatial, 'chan', split_axis=1, concat_axis=0, tiled=True)  117 us
    ppermute x3, waiting for transfers between devices, on_device(): part = lax.ppermute(part, 'chan', [(d, d ^ mask) for d in range(ways)])  94.6 us
    dot_general x1, matrix products, on_device(): lax.dot_general(lax.all_gather(up_weight, ('tile', 'chan'), axis=1, tiled...  92.7 us
    add x1, other arithmetic, on_device(): lon_sum + lon_taps[kernel_tap_index][:, None, None] * sliding_window  32.8 us
    dot_general x4, matrix products, on_device(): jnp.einsum('dts,tsc->dc', down_groups[:, :, group, :], hidden_groups[:, g...  25.4 us
    convert_element_type x2, local copies, waits for them, and re-layouts, layer_norm(): as_float = values.astype(jnp.float32)  24.3 us
    convert_element_type x1, local copies, waits for them, and re-layouts, on_device(): hidden = jax.nn.gelu(expanded, approximate=False).astype(jnp.bfloat16)  22.3 us
    unnamed x23, local copies, waits for them, and re-layouts  18.5 us
  transfers between devices with their start and end apart: 8, of which 4 were waited for; matrix products, arithmetic and copies ran while one was open for 42% of the time, Pallas kernels for 0%

profile of v1, /device:TPU:8, one launch (start us, length us, event | category | flops | bytes accessed | tf_op | source)
XLA Modules:
  0.0 535.4 jit_solution(8554043133220136035)
XLA Ops:
  6.5 2.6 fusion.56
  9.1 1.3 copy.51
  10.5 1.3 copy.52
  11.8 1.8 collective-permute-start.1
  13.6 0.6 fusion.58
  14.2 1.0 fusion.57
  15.2 6.2 %copy.29 = bf16[192,32,360]{2,0,1:T(8,128)(2,1)} copy(bf16[192,32,360]{2,1,0:T(8,128)(2,1)} %param.6) | data formatting | bytes 8847360 | tf_op args[0]
  21.4 0.8 copy.31
  22.2 1.5 copy.35
  23.8 32.8 %fusion.22 = f32[192,32,360]{2,0,1:T(8,128)S(1)} fusion(bf16[192,32,360]{2,0,1:T(8,128)(2,1)} %copy.29, bf16[192,32,8]{2,0,1:T(8,128)(2,1)} %copy.35, bf16[192,32,8]{2,0,1:T(8,128)(2,1)S(1)} %copy.31, f32[192]{0:T(256)S(1)} %bitcast.197, f32[192]{0:T(256)S(1)} %bitcast.198, f32[192]{0:T(256)S(1)} %bitcast.191, f32[192]{0:T(256)S(1)} %bitcast.192, ...), kind=kLoop, calls=%fused_computation.38 | loop fusion | flops 110592000 | bytes 13474560 | tf_op jit(solution)/shard_map/add | solution.py:40
  56.6 10.9 %fusion.33 = bf16[192,32,360]{2,0,1:T(8,128)(2,1)} fusion(f32[192,32,360]{2,0,1:T(8,128)S(1)} %fusion.22, f32[192]{0:T(256)S(1)} %bitcast.188, f32[192]{0:T(256)S(1)} %bitcast.189, f32[192]{0:T(256)S(1)} %bitcast.182, f32[192]{0:T(256)S(1)} %bitcast.183, f32[192]{0:T(256)S(1)} %bitcast.184, f32[192]{0:T(256)S(1)} %bitcast.185, f32[192]{0:T(256)S(1)} %bitcast.186, ...), kind=kLoop, calls=%fused_computation.49 | loop fusion | flops 39813120 | bytes 13277952 | tf_op jit(solution)/shard_map/convert_element_type | solution.py:53
  67.5 5.3 all-to-all-start
  72.8 13.1 %all-gather.5.cloned.1.call-start = ((), (), s32[]{:S(2)}) async-start(), calls=%async_computation.2 | async-start | bytes 5013504 | tf_op jit(solution)/shard_map/all_gather | solution.py:67
  85.9 116.8 %all-to-all-done = bf16[192,32,360]{2,0,1:T(8,128)(2,1)} async-done(((bf16[192,32,360]{2,0,1:T(8,128)(2,1)}), bf16[192,32,360]{2,0,1:T(8,128)(2,1)}, u32[]{:S(2)}, u32[]{:S(2)}) %all-to-all-start) | async-done | bytes 4423712 | tf_op jit(solution)/shard_map/all_to_all | solution.py:57
  202.7 3.5 bitcast_convert_fusion.4
  206.3 5.0 fusion.55
  211.3 5.0 multiply_reduce_fusion
  216.4 12.8 %copy.71 = f32[192,4,8,360]{3,2,0,1:T(8,128)} copy(f32[192,4,8,360]{3,0,2,1:T(8,128)} %copy-done) | data formatting | bytes 17694720 | tf_op jit(solution)/shard_map/convert_element_type | solution.py:24
  229.2 0.1 rsqrt.11
  229.3 11.5 %reshape.67 = f32[768,2880]{1,0:T(8,128)} reshape(f32[4,192,8,360]{3,2,1,0:T(8,128)} %bitcast.173) | data formatting | bytes 17694720 | tf_op jit(solution)/shard_map/convert_element_type | solution.py:24
  240.8 7.1 %multiply_convert_fusion.1.clone.4 = bf16[768,2880]{1,0:T(8,128)(2,1)} fusion(f32[768,2880]{1,0:T(8,128)} %reshape.67, f32[768]{0:T(1024)S(1)} %copy-done.3, f32[2880]{0:T(1024)S(1)} %rsqrt.11, f32[2880]{0:T(1024)S(1)} %div.9), kind=kLoop, calls=%fused_computation.59.clone.clone.clone.clone.1 | loop fusion | flops 8847360 | bytes 13297152 | tf_op jit(solution)/shard_map/convert_element_type | solution.py:66
  247.9 92.7 %fusion.2 = bf16[3072,2880]{0,1:T(8,128)(2,1)} fusion(bf16[768,3072]{0,1:T(8,128)(2,1)} %all-gather.3.cloned.1.call-done, bf16[768,2880]{1,0:T(8,128)(2,1)} %multiply_convert_fusion.1.clone.4), kind=kOutput, calls=%fused_computation.3 | convolution fusion | flops 14164623360 | bytes 26836992 | tf_op jit(solution)/shard_map/dot_general | solution.py:60
  340.6 22.3 %copy.37 = bf16[3072,2880]{1,0:T(8,128)(2,1)} copy(bf16[3072,2880]{0,1:T(8,128)(2,1)} %fusion.2) | data formatting | bytes 35389440 | tf_op jit(solution)/shard_map/convert_element_type | solution.py:66
  362.8 8.7 %fusion.51 = bf16[768,2880]{0,1:T(8,128)(2,1)} fusion(bf16[4,4,192,2880]{3,2,1,0:T(8,128)(2,1)} %bitcast.177, bf16[768,4,4,192]{0,3,2,1:T(8,128)(2,1)} %bitcast.199), kind=kOutput, calls=%fused_computation.89 | convolution fusion | flops 3399598080 | bytes 10125312 | tf_op jit(solution)/shard_map/dts,tsc->dc/dot_general | solution.py:73
  371.5 0.1 copy-done.1
  371.7 1.9 copy-done.5
  373.6 5.5 %fusion.52 = bf16[768,2880]{0,1:T(8,128)(2,1)} fusion(bf16[4,4,192,2880]{3,2,1,0:T(8,128)(2,1)S(1)} %bitcast.178, bf16[768,4,4,192]{0,3,2,1:T(8,128)(2,1)S(1)} %bitcast.200), kind=kOutput, calls=%fused_computation.90 | convolution fusion | flops 3399598080 | bytes 10125312 | tf_op jit(solution)/shard_map/dts,tsc->dc/dot_general | solution.py:73
  379.2 5.5 %fusion.53 = bf16[768,2880]{0,1:T(8,128)(2,1)} fusion(bf16[4,4,192,2880]{3,2,1,0:T(8,128)(2,1)S(1)} %bitcast.179, bf16[768,4,4,192]{0,3,2,1:T(8,128)(2,1)S(1)} %bitcast.201), kind=kOutput, calls=%fused_computation.91 | convolution fusion | flops 3399598080 | bytes 10125312 | tf_op jit(solution)/shard_map/dts,tsc->dc/dot_general | solution.py:73
  384.6 5.7 %fusion.54 = bf16[768,2880]{0,1:T(8,128)(2,1)} fusion(bf16[4,4,192,2880]{3,2,1,0:T(8,128)(2,1)S(1)} %bitcast.180, bf16[768,4,4,192]{0,3,2,1:T(8,128)(2,1)S(1)} %bitcast.202), kind=kOutput, calls=%fused_computation.92 | convolution fusion | flops 3399598080 | bytes 10125312 | tf_op jit(solution)/shard_map/dts,tsc->dc/dot_general | solution.py:73
  390.3 10.3 %add_convert_fusion = bf16[768,2880]{0,1:T(8,128)(2,1)} fusion(bf16[768,2880]{0,1:T(8,128)(2,1)} %fusion.54, bf16[768,2880]{0,1:T(8,128)(2,1)} %fusion.53, bf16[768,2880]{0,1:T(8,128)(2,1)} %fusion.52, bf16[768,2880]{0,1:T(8,128)(2,1)} %fusion.51), kind=kLoop, calls=%fused_computation.64 | loop fusion | flops 17694720 | bytes 22118400 | tf_op jit(solution)/shard_map/convert_element_type | solution.py:81
  400.7 8.0 %constant_dynamic-slice_fusion = (bf16[192,8,360]{0,2,1:T(8,128)(2,1)S(1)}, bf16[192,8,360]{0,2,1:T(8,128)(2,1)}, bf16[192,8,360]{0,2,1:T(8,128)(2,1)}, bf16[192,8,360]{0,2,1:T(8,128)(2,1)S(1)}) fusion(bf16[768,8,360]{0,2,1:T(8,128)(2,1)} %bitcast.176, s32[]{:T(128)S(6)} %select_n.30, s32[]{:T(128)S(6)} %select_n.28, s32[]{:T(128)S(6)} %select_n.26, ...), kind=kLoop, calls=%fused_computation.100 | loop fusion | bytes 8847376 | tf_op jit(solution)/shard_map/dynamic_slice | solution.py:90
  408.7 2.5 copy.62
  411.2 3.4 collective-permute-start.2
  414.6 2.5 copy.63
  417.1 0.1 collective-permute-start.3
  417.2 1.5 copy.64
  418.7 1.4 collective-permute-start.4
  420.1 1.1 copy.61
  421.2 0.7 broadcast_in_dim.2
  421.9 0.2 constant_dynamic-update-slice_fusion.3
  422.2 38.8 %collective-permute-done.2 = bf16[192,8,360]{2,0,1:T(8,128)(2,1)} collective-permute-done((bf16[192,8,360]{2,0,1:T(8,128)(2,1)}, bf16[192,8,360]{2,0,1:T(8,128)(2,1)}, u32[]{:S(2)}, u32[]{:S(2)}) %collective-permute-start.2) | collective-permute-done | bytes 1105952 | tf_op jit(solution)/shard_map/ppermute | solution.py:92
  461.0 1.5 constant_dynamic-update-slice_fusion.2
  462.5 32.0 %collective-permute-done.3 = bf16[192,8,360]{2,0,1:T(8,128)(2,1)} collective-permute-done((bf16[192,8,360]{2,0,1:T(8,128)(2,1)}, bf16[192,8,360]{2,0,1:T(8,128)(2,1)}, u32[]{:S(2)}, u32[]{:S(2)}) %collective-permute-start.3) | collective-permute-done | bytes 1105952 | tf_op jit(solution)/shard_map/ppermute | solution.py:92
  494.5 1.5 constant_dynamic-update-slice_fusion.1
  496.0 23.7 %collective-permute-done.4 = bf16[192,8,360]{2,0,1:T(8,128)(2,1)} collective-permute-done((bf16[192,8,360]{2,0,1:T(8,128)(2,1)}, bf16[192,8,360]{2,0,1:T(8,128)(2,1)}, u32[]{:S(2)}, u32[]{:S(2)}) %collective-permute-start.4) | collective-permute-done | bytes 1105952 | tf_op jit(solution)/shard_map/ppermute | solution.py:92
  519.7 1.5 constant_dynamic-update-slice_fusion
  521.3 2.0 fusion.23
  523.3 5.0 copy.50
  (26 shorter events, 0.2 us)
Async XLA Ops:
  6.5 7.1 %copy-start.2 = (f32[9,192]{1,0:T(8,128)S(1)}, f32[9,192]{1,0:T(8,128)}, u32[]{:S(2)}) copy-start(f32[9,192]{1,0:T(8,128)} %param.7) | copy-start | bytes 20740
  6.5 241.4 %all-gather.3.cloned.1.call-start = ((), (), s32[]{:S(2)}) async-start(), calls=%async_computation.1 | async-start | bytes 5013504 | tf_op jit(solution)/shard_map/all_gather | solution.py:61
  10.4 11.0 %collective-permute-start = (bf16[192,32,8]{0,2,1:T(8,128)(2,1)S(1)}, bf16[192,32,8]{0,2,1:T(8,128)(2,1)S(1)}, u32[]{:S(2)}, u32[]{:S(2)}) collective-permute-start(bf16[192,32,8]{0,2,1:T(8,128)(2,1)S(1)} %copy.51), channel_id=1, source_target_pairs={{0,4},{4,8},{8,12},{12,0},{1,5},{5,9},{9,13},{13,1},{2,6},{6,10},{... | collective-permute-start | bytes 294920 | tf_op jit(solution)/shard_map/ppermute | solution.py:17
  11.8 10.4 %collective-permute-start.1 = (bf16[192,32,8]{0,2,1:T(8,128)(2,1)S(1)}, bf16[192,32,8]{0,2,1:T(8,128)(2,1)S(1)}, u32[]{:S(2)}, u32[]{:S(2)}) collective-permute-start(bf16[192,32,8]{0,2,1:T(8,128)(2,1)S(1)} %copy.52), channel_id=1, source_target_pairs={{4,0},{8,4},{12,8},{0,12},{5,1},{9,5},{13,9},{1,13},{6,2},{10,6},{... | collective-permute-start | bytes 294920 | tf_op jit(solution)/shard_map/ppermute | solution.py:18
  14.2 9.6 %copy-start.4 = (f32[1,192]{1,0:T(1,128)S(1)}, f32[1,192]{1,0:T(1,128)}, u32[]{:S(2)}) copy-start(f32[1,192]{1,0:T(1,128)} %get-tuple-element.28) | copy-start | bytes 2308
  67.5 135.2 %all-to-all-start = ((bf16[192,32,360]{2,0,1:T(8,128)(2,1)}), bf16[192,32,360]{2,0,1:T(8,128)(2,1)}, u32[]{:S(2)}, u32[]{:S(2)}) async-start(bf16[192,32,360]{2,0,1:T(8,128)(2,1)} %fusion.33), calls=%async_computation | async-start | bytes 9437184 | tf_op jit(solution)/shard_map/all_to_all | solution.py:57
  72.8 290.0 %all-gather.5.cloned.1.call-start = ((), (), s32[]{:S(2)}) async-start(), calls=%async_computation.2 | async-start | bytes 5013504 | tf_op jit(solution)/shard_map/all_gather | solution.py:67
  206.2 5.0 copy-start
  229.2 11.6 %copy-start.3 = (f32[768]{0:T(1024)S(1)}, f32[768]{0:T(1024)}, u32[]{:S(2)}) copy-start(f32[768]{0:T(1024)} %param.9) | copy-start | bytes 9220
  362.8 8.8 %copy-start.1 = (bf16[3072,2880]{1,0:T(8,128)(2,1)S(1)}, bf16[3072,2880]{1,0:T(8,128)(2,1)}, u32[]{:S(2)}) copy-start(bf16[3072,2880]{1,0:T(8,128)(2,1)} %copy.37) | copy-start | bytes 53084164
  362.8 10.8 %copy-start.5 = (bf16[768,3072]{0,1:T(8,128)(2,1)S(1)}, bf16[768,3072]{0,1:T(8,128)(2,1)}, u32[]{:S(2)}) copy-start(bf16[768,3072]{0,1:T(8,128)(2,1)} %all-gather.5.cloned.1.call-done) | copy-start | bytes 14155780
  411.2 49.8 %collective-permute-start.2 = (bf16[192,8,360]{2,0,1:T(8,128)(2,1)}, bf16[192,8,360]{2,0,1:T(8,128)(2,1)}, u32[]{:S(2)}, u32[]{:S(2)}) collective-permute-start(bf16[192,8,360]{2,0,1:T(8,128)(2,1)} %copy.62), channel_id=1, source_target_pairs={{0,1},{1,0},{2,3},{3,2},{4,5},{5,4},{6,7},{7,6},{8,9},{9,8},{10,11... | collective-permute-start | bytes 3317768 | tf_op jit(solution)/shard_map/ppermute | solution.py:92
  417.1 77.4 %collective-permute-start.3 = (bf16[192,8,360]{2,0,1:T(8,128)(2,1)}, bf16[192,8,360]{2,0,1:T(8,128)(2,1)}, u32[]{:S(2)}, u32[]{:S(2)}) collective-permute-start(bf16[192,8,360]{2,0,1:T(8,128)(2,1)} %copy.63), channel_id=1, source_target_pairs={{0,2},{1,3},{2,0},{3,1},{4,6},{5,7},{6,4},{7,5},{8,10},{9,11},{10,... | collective-permute-start | bytes 3317768 | tf_op jit(solution)/shard_map/ppermute | solution.py:92
  417.2 104.0 %slice-start = ((s8[4718592]{0:T(1024)(128)(4,1)}), s8[524288]{0:T(1024)(128)(4,1)S(1)}, s32[]{:S(2)}) async-start(s8[4718592]{0:T(1024)(128)(4,1)} %bitcast.174), calls=%async_computation.3 | async-start | bytes 1048576
  418.7 101.0 %collective-permute-start.4 = (bf16[192,8,360]{2,0,1:T(8,128)(2,1)}, bf16[192,8,360]{2,0,1:T(8,128)(2,1)}, u32[]{:S(2)}, u32[]{:S(2)}) collective-permute-start(bf16[192,8,360]{2,0,1:T(8,128)(2,1)} %copy.64), channel_id=1, source_target_pairs={{0,3},{1,2},{2,1},{3,0},{4,7},{5,6},{6,5},{7,4},{8,11},{9,10},{10,... | collective-permute-start | bytes 3317768 | tf_op jit(solution)/shard_map/ppermute | solution.py:92
  421.2 100.1 %slice-start.1 = ((s8[4718592]{0:T(1024)(128)(4,1)}), s8[4194304]{0:T(1024)(128)(4,1)S(1)}, s32[]{:S(2)}) async-start(s8[4718592]{0:T(1024)(128)(4,1)} %bitcast.174), calls=%async_computation.4 | async-start | bytes 8388608
Sparse Core Ops, SparseCore 0:
  13.7 54.5 all-gather.2
  86.0 111.4 all-gather.4
